TPU v7x, 32 devices: a whole 2x2x4 slice. The times are simulated.
32 devices in a mesh: dp: 4 (over x, core), seq: 8 (over z, y).
Axes of the slice: x: 2, y: 2, z: 4, core: 2. Of those that a mesh axis runs over, the one named last changes fastest.
Arguments:
- spatial_input: bfloat16 [4, 8, 64, 256], P('dp', 'seq'), may hold values from -6 to 6
- temporal_input: bfloat16 [4, 64, 8, 256], P('dp', 'seq'), may hold values from -6 to 6
- out_cotangent: bfloat16 [4, 8, 64, 256], P('dp', 'seq'), may hold values from -6 to 6
- weights: bfloat16 [2, 256, 1024], replicated, may hold values from -3 to 3
- gains: float32 [2, 256], replicated, may hold values from 0.1 to 1.9
Outputs:
- input_grad: bfloat16 [4, 8, 64, 256], P('dp', 'seq')
- weight_grads: float32 [2, 262144], P(None, ('dp', 'seq'))
- gain_grads: float32 [2, 256], replicated
All inputs are finite; a program needn't handle non-finite values.
Results may differ from a plain program's by a relative error of at most 0.023.
Values may be sent and summed in bfloat16 or wider, within the bound.
A program may use at most 64 MiB of HBM per device.

v0:
```python
from functools import partial
import math
import jax
import jax.numpy as jnp
from jax import lax
from jax.sharding import PartitionSpec as P

HEADS = 4


def one_head(head_parts, score_scale):
    query_rows, key_rows, value_rows = head_parts
    scores = (
        jnp.einsum("gqe,gke->gqk", query_rows, key_rows, preferred_element_type=jnp.float32)
        * score_scale
    )
    probs = jax.nn.softmax(scores, axis=-1).astype(jnp.bfloat16)
    return jnp.einsum("gqk,gke->gqe", probs, value_rows, preferred_element_type=jnp.float32).astype(
        jnp.bfloat16
    )


def attend_block(block_input, gain_vector, weight, head_count):
    groups, length, model_width = block_input.shape
    head_size = model_width // head_count
    mean_sq = jnp.mean(block_input * block_input, axis=-1, keepdims=True)
    normed = (block_input * lax.rsqrt(mean_sq + 1e-06) * gain_vector).astype(jnp.bfloat16)
    w_cast = weight.astype(jnp.bfloat16)
    packed = jnp.dot(
        normed.reshape(groups * length, model_width),
        w_cast[:, : 3 * model_width],
        preferred_element_type=jnp.float32,
    ).astype(jnp.bfloat16)
    packed = jnp.transpose(
        packed.reshape(groups, length, 3, head_count, head_size), (2, 3, 0, 1, 4)
    )
    head_fn = jax.checkpoint(partial(one_head, score_scale=1.0 / math.sqrt(head_size)))
    mixed_heads = lax.map(head_fn, (packed[0], packed[1], packed[2]))
    mixed_heads = jnp.transpose(mixed_heads, (1, 2, 0, 3)).reshape(groups * length, model_width)
    result = jnp.dot(mixed_heads, w_cast[:, 3 * model_width :], preferred_element_type=jnp.float32)
    return result.reshape(groups, length, model_width)


def per_device(spatial_input, temporal_input, out_cotangent, weights, gains):
    w_float = weights.astype(jnp.float32)
    block_fn = partial(attend_block, head_count=HEADS)
    sample_count = spatial_input.shape[0] * lax.axis_size("dp")
    frame_count = spatial_input.shape[1] * lax.axis_size("seq")
    patch_count = spatial_input.shape[2]
    grad_factor = 1.0 / math.sqrt(sample_count * frame_count * patch_count)
    patch_major = jnp.swapaxes(out_cotangent[0], 0, 1)
    temporal_cot = lax.all_to_all(
        patch_major, "seq", split_axis=0, concat_axis=1, tiled=True
    ).astype(jnp.float32)
    unused_t, pullback_t = jax.vjp(
        block_fn, temporal_input[0].astype(jnp.float32), gains[1], w_float[1]
    )
    grad_ut, grad_gt, grad_wt = pullback_t(temporal_cot)
    temporal_term = (grad_wt * grad_factor).reshape(1, -1)
    mid_grad = (temporal_cot + grad_ut).astype(jnp.bfloat16)
    frame_back = lax.all_to_all(mid_grad, "seq", split_axis=1, concat_axis=0, tiled=True)
    spatial_cot = jnp.swapaxes(frame_back, 0, 1).astype(jnp.float32)
    unused_s, pullback_s = jax.vjp(
        block_fn, spatial_input[0].astype(jnp.float32), gains[0], w_float[0]
    )
    grad_us, grad_gs, grad_ws = pullback_s(spatial_cot)
    input_grad = (spatial_cot + grad_us).astype(jnp.bfloat16)[None]
    spatial_term = (grad_ws * grad_factor).reshape(1, -1)
    both_terms = jnp.concatenate([spatial_term, temporal_term], axis=0)
    grid_terms = both_terms.reshape(2, lax.axis_size("dp"), lax.axis_size("seq"), -1)
    over_frames = lax.psum_scatter(
        grid_terms.astype(jnp.bfloat16), "seq", scatter_dimension=2, tiled=True
    ).astype(jnp.float32)
    over_frames = over_frames.reshape(2, lax.axis_size("dp"), -1)
    weight_grads = (
        lax.psum_scatter(over_frames.astype(jnp.bfloat16), "dp", scatter_dimension=1, tiled=True)
        .astype(jnp.float32)
        .reshape(2, -1)
    )
    gain_grads = lax.psum(jnp.stack([grad_gs, grad_gt]) * grad_factor, ("dp", "seq"))
    return (input_grad, weight_grads, gain_grads)


def solution(mesh):
    return jax.shard_map(
        per_device,
        mesh=mesh,
        in_specs=(
            P("dp", "seq", None, None),
            P("dp", "seq", None, None),
            P("dp", "seq", None, None),
            P(),
            P(),
        ),
        out_specs=(P("dp", "seq", None, None), P(None, ("dp", "seq")), P()),
        check_vma=False,
    )
```

profile of v0, /device:TPU:0, one launch (start us, length us, event | category | flops | bytes accessed | tf_op | source)
XLA Modules:
  0.0 179.6 jit_solution(7019148246470243943)
XLA Ops:
  7.2 0.5 broadcast.288
  7.7 1.4 reduce.34
  9.1 0.6 reshape.395
  9.7 7.4 %all-to-all-start = ((bf16[8,2,1024]{2,1,0:T(2,128)(2,1)}), bf16[8,2,1024]{2,1,0:T(2,128)(2,1)S(1)}, u32[]{:S(2)}, u32[]{:S(2)}) async-start(bf16[8,2,1024]{2,1,0:T(2,128)(2,1)} %reshape.395), calls=%async_computation | async-start | bytes 65536 | tf_op jit(solution)/shard_map/all_to_all | solution.py:52
  17.3 0.7 copy-done.1
  18.1 0.6 copy-done.2
  18.9 1.3 slice_bitcast_fusion.1
  20.6 2.0 %while.59 = (s32[]{:T(128)}, bf16[4,8,8,64]{3,2,1,0:T(8,128)(2,1)S(1)}, bf16[4,8,8,64]{3,2,1,0:T(8,128)(2,1)S(1)}, bf16[4,8,8,64]{3,2,1,0:T(8,128)(2,1)S(1)}, bf16[4,8,8,64]{3,2,1,0:T(8,128)(2,1)S(1)}, /*index=5*/s32[]{:T(128)}) while((s32[]{:T(128)}, bf16[4,8,8,64]{3,2,1,0:T(8,128)(2,1)S(1)}, bf16[4,8,8,64]{3,2,1,0:T(8,128)(2,1)S(1)}, ...), condition=%wide.region_21.22_spmd, body=%wide.region_18.0_spmd.sunk | while | flops 204368 | bytes 105805 | solution.py:38
  20.8 0.3 fusion.234
  21.3 0.3 fusion.234
  21.8 0.3 fusion.234
  22.3 0.3 fusion.234
  23.1 1.6 while.58
  25.6 4.9 %while.56 = (s32[]{:T(128)}, bf16[4,8,8,64]{3,2,1,0:T(8,128)(2,1)S(1)}, bf16[4,8,8,64]{3,2,1,0:T(8,128)(2,1)S(1)}, bf16[4,8,8,64]{3,2,1,0:T(8,128)(2,1)S(1)}, bf...) while((s32[]{:T(128)}, ...), condition=%wide.region_5.6_spmd, body=%wide.region_1.5_spmd.sunk | while | flops 549215 | bytes 388997 | solution.py:38
  25.9 0.3 fusion.215
  26.2 0.3 fusion.214
  26.5 0.3 fusion.213
  27.2 0.3 fusion.215
  27.4 0.3 fusion.214
  27.7 0.3 fusion.213
  28.4 0.3 fusion.215
  28.6 0.3 fusion.214
  28.9 0.3 fusion.213
  29.6 0.3 fusion.215
  29.9 0.3 fusion.214
  30.1 0.3 fusion.213
  30.9 0.3 fusion.84
  31.3 0.7 fusion.99
  32.0 6.0 %all-to-all-start.1 = ((bf16[8,8,256]{2,0,1:T(8,128)(2,1)}), bf16[8,8,256]{2,0,1:T(8,128)(2,1)S(1)}, u32[]{:S(2)}, u32[]{:S(2)}) async-start(bf16[8,8,256]{2,0,1:T(8,128)(2,1)} %fusion.99), calls=%async_computation.1 | async-start | bytes 65536 | tf_op jit(solution)/shard_map/all_to_all | solution.py:61
  38.2 0.3 convolution_convert_fusion.10
  38.6 0.2 concatenate.10
  38.9 0.4 copy.103
  39.3 5.4 %all-to-all-done.1 = bf16[8,8,256]{2,0,1:T(8,128)(2,1)S(1)} async-done(((bf16[8,8,256]{2,0,1:T(8,128)(2,1)}), bf16[8,8,256]{2,0,1:T(8,128)(2,1)S(1)}, u32[]{:S(2)}, u32[]{:S(2)}) %all-to-all-start.1) | async-done | bytes 32800 | tf_op jit(solution)/shard_map/all_to_all | solution.py:61
  45.0 4.7 %while.57 = (s32[]{:T(128)}, bf16[4,1,64,64]{2,3,0,1:T(8,128)(2,1)S(1)}, bf16[4,1,64,64]{2,3,0,1:T(8,128)(2,1)S(1)}, bf16[4,1,64,64]{2,3,1,0:T(8,128)(2,1)S(1)},...) while((s32[]{:T(128)}, ...), condition=%wide.region_12.13_spmd, body=%wide.region_8.12_spmd.sunk | while | flops 2727939 | bytes 431237 | solution.py:38
  49.8 0.4 convolution_convert_fusion.11
  50.4 0.2 concatenate.9
  50.7 0.4 copy.102
  51.1 1.7 pad_maximum_fusion
  52.9 0.6 copy-done.4
  53.6 0.6 dynamic-slice.2
  54.2 0.6 dynamic-slice
  54.8 0.4 fusion.97
  55.2 0.7 fusion.117
  55.9 72.8 %all-reduce.15.cloned.1.call-done = bf16[2,4,8,8192]{3,1,0,2:T(4,128)(2,1)} async-done(((bf16[2,4,8,8192]{3,1,0,2:T(4,128)(2,1)}), bf16[2,4,8,8192]{3,1,0,2:T(4,128)(2,1)}) %all-reduce.15.cloned.1.call-update) | async-done | bytes 1048592
  128.7 1.6 dynamic-slice_bitcast_fusion.8
  130.3 0.8 copy.104
  131.1 39.6 %psum.7 = f32[2,256]{1,0:T(2,128)} all-reduce(f32[2,256]{1,0:T(2,128)S(1)} %maximum_multiply_fusion), channel_id=1, replica_groups=mesh['dp'=4,'seq'=8] {'dp','seq'}, use_global_device_ids=true, to_apply=%region_26.27 | all-reduce | flops 512 | bytes 4096 | tf_op jit(solution)/shard_map/psum | solution.py:80
  170.7 2.0 %bitcast_convert_fusion = f32[2,8192]{1,0:T(2,128)} fusion(bf16[2,4,8192]{2,0,1:T(2,128)(2,1)} %all-reduce.17.cloned.1.call-done, u32[]{:T(128)} %bitcast.79), kind=kLoop, calls=%fused_computation.171 | loop fusion | flops 16384 | bytes 98308 | tf_op jit(solution)/shard_map/reshape | solution.py:78
  (158 shorter events, 11.6 us)
Async XLA Ops:
  9.7 7.4 %copy-start = (bf16[1,8,8,256]{3,2,1,0:T(8,128)(2,1)S(1)}, bf16[1,8,8,256]{3,2,1,0:T(8,128)(2,1)}, u32[]{:S(2)}) copy-start(bf16[1,8,8,256]{3,2,1,0:T(8,128)(2,1)} %param.14) | copy-start | bytes 98308
  9.7 15.4 %all-to-all-start = ((bf16[8,2,1024]{2,1,0:T(2,128)(2,1)}), bf16[8,2,1024]{2,1,0:T(2,128)(2,1)S(1)}, u32[]{:S(2)}, u32[]{:S(2)}) async-start(bf16[8,2,1024]{2,1,0:T(2,128)(2,1)} %reshape.395), calls=%async_computation | async-start | bytes 65536 | tf_op jit(solution)/shard_map/all_to_all | solution.py:52
  17.3 0.8 copy-start.1
  18.0 0.7 copy-start.2
  32.0 12.7 %all-to-all-start.1 = ((bf16[8,8,256]{2,0,1:T(8,128)(2,1)}), bf16[8,8,256]{2,0,1:T(8,128)(2,1)S(1)}, u32[]{:S(2)}, u32[]{:S(2)}) async-start(bf16[8,8,256]{2,0,1:T(8,128)(2,1)} %fusion.99), calls=%async_computation.1 | async-start | bytes 65536 | tf_op jit(solution)/shard_map/all_to_all | solution.py:61
  38.0 90.8 %all-reduce.15.cloned.1.call-start = ((), (), s32[]{:S(2)}) async-start(), calls=%async_computation.2 | async-start | bytes 2097152
  52.9 117.9 %all-reduce.17.cloned.1.call-start = ((), (), s32[]{:S(2)}) async-start(), calls=%async_computation.3 | async-start | bytes 262144
  52.9 0.7 copy-start.4
  53.6 0.7 copy-start.3
Sparse Core Ops, SparseCore 0:
  53.0 75.6 all-reduce.14
  131.2 31.3 all-reduce.16
where the time goes:
time: 180 us
  waiting for transfers between devices  78.2 us (43%)
  blocking collectives  39.6 us (22%)
  between operations  14.4 us (8%)
  matrix products  13.7 us (8%)
  starting transfers between devices  13.5 us (8%)
  local copies, waits for them, and re-layouts  12 us (7%)
  other arithmetic  7.74 us (4%)
    unnamed x4, waiting for transfers between devices  72.8 us
    psum x1, blocking collectives, per_device(): lax.psum(jnp.stack([grad_gs, grad_gt]) * grad_factor, ('dp', 'seq'))  39.6 us
    all_to_all x1, starting transfers between devices, per_device(): lax.all_to_all(patch_major, 'seq', split_axis=0, concat_axis=1, tiled=True)  7.44 us
    all_to_all x1, starting transfers between devices, per_device(): lax.all_to_all(mid_grad, 'seq', split_axis=1, concat_axis=0, tiled=True)  5.99 us
    all_to_all x1, waiting for transfers between devices, per_device(): lax.all_to_all(mid_grad, 'seq', split_axis=1, concat_axis=0, tiled=True)  5.36 us
    dot_general x24, matrix products, one_head(): jnp.einsum('gqk,gke->gqe', probs, value_rows, preferred_element_type=jnp....  5.11 us
    dot_general x24, matrix products, one_head(): jnp.einsum('gqe,gke->gqk', query_rows, key_rows, preferred_element_type=j...  4.94 us
    unnamed x15, local copies, waits for them, and re-layouts  3.85 us
  transfers between devices with their start and end apart: 4, of which 2 were waited for; matrix products, arithmetic and copies ran while one was open for 6% of the time, Pallas kernels for 0%

commit v1 on v0

--- a/solution.py
+++ b/solution.py
@@ -77,7 +77,8 @@
         .astype(jnp.float32)
         .reshape(2, -1)
     )
-    gain_grads = lax.psum(jnp.stack([grad_gs, grad_gt]) * grad_factor, ("dp", "seq"))
+    spread_the_rings = lambda u: lax.all_gather(u, ("dp", "seq")).sum(axis=0)
+    gain_grads = spread_the_rings(jnp.stack([grad_gs, grad_gt]) * grad_factor)
     return (input_grad, weight_grads, gain_grads)
 
 

time: 180 us -> 207 us (1.15)
  blocking collectives: 39.6 us -> 66.2 us
    all_gather x0 -> x1, blocking collectives: none -> 66.2 us  [per_device(): spread_the_rings = lambda u: lax.all_gather(u, ('dp', 'seq')).sum(axis=0)]
    psum x1 -> x0, blocking collectives: 39.6 us -> none  [per_device(): lax.psum(jnp.stack([grad_gs, grad_gt]) * grad_factor, ('dp', 'seq'))]
  transfers between devices with their start and end apart: 4 -> 4, of which waited for: 2 -> 2; matrix products, arithmetic and copies ran while one was open for 6% -> 5% of each run, Pallas kernels for 0% -> 0%
where the time goes in v1:
time: 207 us
  waiting for transfers between devices  78.2 us (38%)
  blocking collectives  66.2 us (32%)
  between operations  14.4 us (7%)
  matrix products  13.7 us (7%)
  starting transfers between devices  13.5 us (7%)
  local copies, waits for them, and re-layouts  12 us (6%)
  other arithmetic  8.36 us (4%)
    unnamed x4, waiting for transfers between devices  72.8 us
    all_gather x1, blocking collectives, per_device(): spread_the_rings = lambda u: lax.all_gather(u, ('dp', 'seq')).sum(axis=0)  66.2 us
    all_to_all x1, starting transfers between devices, per_device(): lax.all_to_all(patch_major, 'seq', split_axis=0, concat_axis=1, tiled=True)  7.44 us
    all_to_all x1, starting transfers between devices, per_device(): lax.all_to_all(mid_grad, 'seq', split_axis=1, concat_axis=0, tiled=True)  5.99 us
    all_to_all x1, waiting for transfers between devices, per_device(): lax.all_to_all(mid_grad, 'seq', split_axis=1, concat_axis=0, tiled=True)  5.36 us
    dot_general x24, matrix products, one_head(): jnp.einsum('gqk,gke->gqe', probs, value_rows, preferred_element_type=jnp....  5.11 us
    dot_general x24, matrix products, one_head(): jnp.einsum('gqe,gke->gqk', query_rows, key_rows, preferred_element_type=j...  4.94 us
  transfers between devices with their start and end apart: 4, of which 2 were waited for; matrix products, arithmetic and copies ran while one was open for 5% of the time, Pallas kernels for 0%

profile of v1, /device:TPU:0, one launch (start us, length us, event | category | flops | bytes accessed | tf_op | source)
XLA Modules:
  0.0 206.9 jit_solution(7113433050615724808)
XLA Ops:
  7.2 0.5 broadcast.295
  7.7 1.4 reduce.34
  9.1 0.6 reshape.426
  9.7 7.4 %all-to-all-start = ((bf16[8,2,1024]{2,1,0:T(2,128)(2,1)}), bf16[8,2,1024]{2,1,0:T(2,128)(2,1)S(1)}, u32[]{:S(2)}, u32[]{:S(2)}) async-start(bf16[8,2,1024]{2,1,0:T(2,128)(2,1)} %reshape.426), calls=%async_computation | async-start | bytes 65536 | tf_op jit(solution)/shard_map/all_to_all | solution.py:52
  17.3 0.7 copy-done.1
  18.1 0.6 copy-done.2
  18.9 1.3 slice_bitcast_fusion.1
  20.6 2.0 while.59
  20.8 0.3 fusion.234
  21.3 0.3 fusion.234
  21.8 0.3 fusion.234
  22.3 0.3 fusion.234
  23.1 1.6 while.58
  25.6 4.9 %while.56 = (s32[]{:T(128)}, bf16[4,8,8,64]{3,2,1,0:T(8,128)(2,1)S(1)}, bf16[4,8,8,64]{3,2,1,0:T(8,128)(2,1)S(1)}, bf16[4,8,8,64]{3,2,1,0:T(8,128)(2,1)S(1)}, bf...) while((s32[]{:T(128)}, ...), condition=%wide.region_5.6_spmd, body=%wide.region_1.5_spmd.sunk | while | flops 549215 | bytes 388997 | solution.py:38
  25.9 0.3 fusion.215
  26.2 0.3 fusion.214
  26.5 0.3 fusion.213
  27.2 0.3 fusion.215
  27.4 0.3 fusion.214
  27.7 0.3 fusion.213
  28.4 0.3 fusion.215
  28.6 0.3 fusion.214
  28.9 0.3 fusion.213
  29.6 0.3 fusion.215
  29.9 0.3 fusion.214
  30.1 0.3 fusion.213
  30.9 0.3 fusion.84
  31.3 0.7 fusion.99
  32.0 6.0 %all-to-all-start.1 = ((bf16[8,8,256]{2,0,1:T(8,128)(2,1)}), bf16[8,8,256]{2,0,1:T(8,128)(2,1)S(1)}, u32[]{:S(2)}, u32[]{:S(2)}) async-start(bf16[8,8,256]{2,0,1:T(8,128)(2,1)} %fusion.99), calls=%async_computation.1 | async-start | bytes 65536 | tf_op jit(solution)/shard_map/all_to_all | solution.py:61
  38.2 0.3 convolution_convert_fusion.10
  38.9 0.4 copy.103
  39.3 5.4 %all-to-all-done.1 = bf16[8,8,256]{2,0,1:T(8,128)(2,1)S(1)} async-done(((bf16[8,8,256]{2,0,1:T(8,128)(2,1)}), bf16[8,8,256]{2,0,1:T(8,128)(2,1)S(1)}, u32[]{:S(2)}, u32[]{:S(2)}) %all-to-all-start.1) | async-done | bytes 32800 | tf_op jit(solution)/shard_map/all_to_all | solution.py:61
  45.0 4.7 %while.57 = (s32[]{:T(128)}, bf16[4,1,64,64]{2,3,0,1:T(8,128)(2,1)S(1)}, bf16[4,1,64,64]{2,3,0,1:T(8,128)(2,1)S(1)}, bf16[4,1,64,64]{2,3,1,0:T(8,128)(2,1)S(1)},...) while((s32[]{:T(128)}, ...), condition=%wide.region_12.13_spmd, body=%wide.region_8.12_spmd.sunk | while | flops 2727939 | bytes 431237 | solution.py:38
  49.8 0.4 convolution_convert_fusion.11
  50.4 0.2 concatenate.16
  50.7 0.4 copy.102
  51.1 1.7 pad_maximum_fusion
  52.9 0.6 copy-done.4
  53.6 0.6 dynamic-slice.2
  54.2 0.6 dynamic-slice
  54.8 0.4 fusion.97
  55.2 0.7 fusion.117
  55.9 72.8 %all-reduce.15.cloned.1.call-done = bf16[2,4,8,8192]{3,1,0,2:T(4,128)(2,1)} async-done(((bf16[2,4,8,8192]{3,1,0,2:T(4,128)(2,1)}), bf16[2,4,8,8192]{3,1,0,2:T(4,128)(2,1)}) %all-reduce.15.cloned.1.call-update) | async-done | bytes 1048592
  128.7 1.6 dynamic-slice_bitcast_fusion.8
  130.3 0.8 copy.104
  131.1 66.2 %all_gather.4 = f32[32,2,256]{2,1,0:T(2,128)S(1)} all-gather(f32[1,2,256]{2,1,0:T(2,128)S(1)} %maximum_multiply_fusion), channel_id=1, replica_groups=mesh['dp'=4,'seq'=8] {'dp','seq'}, dimensions={0}, use_global_device_ids=true | all-gather | bytes 67584 | tf_op jit(solution)/shard_map/all_gather | solution.py:80
  197.4 0.6 reduce_sum.159
  198.0 2.0 bitcast_convert_fusion
  (159 shorter events, 11.8 us)
Async XLA Ops:
  9.7 7.4 %copy-start = (bf16[1,8,8,256]{3,2,1,0:T(8,128)(2,1)S(1)}, bf16[1,8,8,256]{3,2,1,0:T(8,128)(2,1)}, u32[]{:S(2)}) copy-start(bf16[1,8,8,256]{3,2,1,0:T(8,128)(2,1)} %param.14) | copy-start | bytes 98308
  9.7 15.4 %all-to-all-start = ((bf16[8,2,1024]{2,1,0:T(2,128)(2,1)}), bf16[8,2,1024]{2,1,0:T(2,128)(2,1)S(1)}, u32[]{:S(2)}, u32[]{:S(2)}) async-start(bf16[8,2,1024]{2,1,0:T(2,128)(2,1)} %reshape.426), calls=%async_computation | async-start | bytes 65536 | tf_op jit(solution)/shard_map/all_to_all | solution.py:52
  17.3 0.8 copy-start.1
  18.0 0.7 copy-start.2
  32.0 12.7 %all-to-all-start.1 = ((bf16[8,8,256]{2,0,1:T(8,128)(2,1)}), bf16[8,8,256]{2,0,1:T(8,128)(2,1)S(1)}, u32[]{:S(2)}, u32[]{:S(2)}) async-start(bf16[8,8,256]{2,0,1:T(8,128)(2,1)} %fusion.99), calls=%async_computation.1 | async-start | bytes 65536 | tf_op jit(solution)/shard_map/all_to_all | solution.py:61
  38.0 90.8 %all-reduce.15.cloned.1.call-start = ((), (), s32[]{:S(2)}) async-start(), calls=%async_computation.2 | async-start | bytes 2097152
  52.9 145.1 %all-reduce.17.cloned.1.call-start = ((), (), s32[]{:S(2)}) async-start(), calls=%async_computation.3 | async-start | bytes 262144
  52.9 0.7 copy-start.4
  53.6 0.7 copy-start.3
Sparse Core Ops, SparseCore 0:
  53.0 75.6 all-reduce.14
  131.2 31.3 all-reduce.16
